TPU v7x, 512 devices: a whole 4x4x16 slice. The times are simulated.
512 devices in a mesh: seq: 128 (over y, z, core), head: 4 (over x).
Axes of the slice: x: 4, y: 4, z: 16, core: 2. Of those that a mesh axis runs over, the one named last changes fastest.
Arguments:
- queries: bfloat16 [65536, 2048], P('seq', 'head'), may hold values from -6 to 6
- key_vectors: bfloat16 [65536, 2048], P('seq', 'head'), may hold values from -6 to 6
- values: bfloat16 [65536, 2048], P('seq', 'head'), may hold values from -6 to 6
- out_weight: bfloat16 [2048, 2048], P('head', 'seq'), may hold values from -4 to 4
Outputs:
- mixed: bfloat16 [65536, 2048], P('seq', 'head')
All inputs are finite; a program needn't handle non-finite values.
Results may differ from a plain program's by a relative error of at most 0.0095.
Values may be sent and summed in bfloat16 or wider, within the bound.
No kernel may reach another device: no remote copies, remote signals or barrier semaphores. Data moves between devices by JAX's collectives and lax.ppermute only.
A program may use at most 64 MiB of HBM per device.

v0:
```python
import math
import jax
import jax.numpy as jnp
from jax import lax
from jax.sharding import PartitionSpec as P

HEAD_DIM = 128
BLOCK = 128
LEVELS = 5


def partner(value, axis, stride):
    mask = 2**stride
    pairs = [(source, source ^ mask) for source in range(lax.axis_size(axis))]
    return lax.ppermute(value, axis, pairs)


def pool_mean(array_in):
    paired = array_in.astype(jnp.float32).reshape(array_in.shape[0] // 2, 2, array_in.shape[1])
    return ((paired[:, 0] + paired[:, 1]) * 0.5).astype(jnp.bfloat16)


def pool_sum(array_in):
    paired = array_in.astype(jnp.float32).reshape(array_in.shape[0] // 2, 2, array_in.shape[1])
    return (paired[:, 0] + paired[:, 1]).astype(jnp.bfloat16)


def to_blocks(array_in, head_count, block_rows):
    return array_in.reshape(-1, block_rows, head_count, array_in.shape[1] // head_count)


def swap_pairs(blocked):
    block_count = blocked.shape[0]
    return blocked.reshape((block_count // 2, 2) + blocked.shape[1:])[:, ::-1].reshape(
        blocked.shape
    )


def level_terms(
    blocked_query_rows, blocked_key_rows, blocked_value_rows, weight, logit_scale_factor
):
    attention_logits = (
        jnp.einsum(
            "bqhd,bkhd->bhqk",
            blocked_query_rows,
            blocked_key_rows,
            preferred_element_type=jnp.float32,
        )
        * logit_scale_factor
    )
    peak_score = jnp.max(attention_logits, axis=-1)
    expo = jnp.exp(attention_logits - peak_score[..., None])
    mass = weight * jnp.sum(expo, axis=-1)
    weighted_value_sum = jnp.einsum(
        "bhqk,bkhd->bqhd",
        expo.astype(jnp.bfloat16),
        blocked_value_rows,
        preferred_element_type=jnp.float32,
    )
    head_count = blocked_query_rows.shape[2]
    peak_rows = jnp.transpose(peak_score, (0, 2, 1)).reshape(-1, head_count)
    mass_rows = jnp.transpose(mass, (0, 2, 1)).reshape(-1, head_count)
    return (
        peak_rows,
        mass_rows,
        weighted_value_sum.reshape(-1, head_count, weighted_value_sum.shape[3]),
    )


def merge_level(running, terms, factor):
    running_max, running_sum, running_out = running
    peak_rows = jnp.repeat(terms[0], factor, axis=0)
    mass_rows = jnp.repeat(terms[1], factor, axis=0)
    weighted_value_sum = jnp.repeat(terms[2], factor, axis=0)
    newest = jnp.maximum(running_max, peak_rows)
    keep_old = jnp.exp(running_max - newest)
    keep_new = jnp.exp(peak_rows - newest)
    return (
        newest,
        running_sum * keep_old + mass_rows * keep_new,
        running_out * keep_old[..., None] + weighted_value_sum * keep_new[..., None],
    )


def body(queries, key_vectors, values, out_weight):
    row_count, col_count = queries.shape
    head_count = col_count // HEAD_DIM
    logit_scale_factor = 1.0 / math.sqrt(HEAD_DIM)
    seq_index = lax.axis_index("seq")
    blocked_key_rows = to_blocks(key_vectors, head_count, BLOCK)
    blocked_value_rows = to_blocks(values, head_count, BLOCK)
    near_keys = jnp.concatenate([blocked_key_rows, swap_pairs(blocked_key_rows)], axis=1)
    near_values = jnp.concatenate([blocked_value_rows, swap_pairs(blocked_value_rows)], axis=1)
    running = level_terms(
        to_blocks(queries, head_count, BLOCK), near_keys, near_values, 1.0, logit_scale_factor
    )
    level_queries, level_keys, level_values = (queries, key_vectors, values)
    far_keys, far_values = (key_vectors, values)
    is_local = True
    partner_bit = 0
    for coarse_level in range(1, LEVELS + 1):
        level_queries = pool_mean(level_queries)
        if is_local:
            level_keys = pool_mean(level_keys)
            level_values = pool_sum(level_values)
            is_local = level_keys.shape[0] >= 2 * BLOCK
        else:
            leading = seq_index >> partner_bit - 1 & 1 == 0
            level_keys = pool_mean(
                jnp.concatenate(
                    [
                        jnp.where(leading, level_keys, far_keys),
                        jnp.where(leading, far_keys, level_keys),
                    ],
                    axis=0,
                )
            )
            level_values = pool_sum(
                jnp.concatenate(
                    [
                        jnp.where(leading, level_values, far_values),
                        jnp.where(leading, far_values, level_values),
                    ],
                    axis=0,
                )
            )
        if is_local:
            blocked_key_rows = swap_pairs(to_blocks(level_keys, head_count, BLOCK))
            blocked_value_rows = swap_pairs(to_blocks(level_values, head_count, BLOCK))
        else:
            far_keys, far_values = partner((level_keys, level_values), "seq", partner_bit)
            partner_bit += 1
            blocked_key_rows = to_blocks(far_keys, head_count, BLOCK)
            blocked_value_rows = to_blocks(far_values, head_count, BLOCK)
        blocked_query_rows = to_blocks(
            level_queries, head_count, level_queries.shape[0] // blocked_key_rows.shape[0]
        )
        terms = level_terms(
            blocked_query_rows,
            blocked_key_rows,
            blocked_value_rows,
            2.0**coarse_level,
            logit_scale_factor,
        )
        running = merge_level(running, terms, 2**coarse_level)
    attended = (
        (running[2] / running[1][..., None]).reshape(row_count, col_count).astype(jnp.bfloat16)
    )
    partial_terms = jnp.dot(
        attended,
        lax.all_gather(out_weight, "seq", axis=1, tiled=True),
        preferred_element_type=jnp.float32,
    )
    rounded_terms = partial_terms.astype(jnp.bfloat16).astype(jnp.float32)
    mixed = lax.psum_scatter(
        rounded_terms.astype(jnp.bfloat16), "head", scatter_dimension=1, tiled=True
    )
    return mixed


def solution(mesh):
    in_specs = (P("seq", "head"), P("seq", "head"), P("seq", "head"), P("head", "seq"))
    out_specs = P("seq", "head")
    return jax.shard_map(body, mesh=mesh, in_specs=in_specs, out_specs=out_specs, check_vma=False)
```

profile of v0, /device:TPU:1, one launch (start us, length us, event | category | flops | bytes accessed | tf_op | source)
XLA Modules:
  0.0 223.5 jit_solution(2739491692825542733)
XLA Ops:
  7.3 1.7 reshape.785
  9.0 0.8 fusion.104
  10.7 8.7 %collective-permute-start = (bf16[128,512]{1,0:T(8,128)(2,1)S(1)}, bf16[128,512]{1,0:T(8,128)(2,1)}, u32[]{:S(2)}, u32[]{:S(2)}) collective-permute-start(bf16[128,512]{1,0:T(8,128)(2,1)S(1)} %fusion.53), channel_id=1, source_target_pairs={{0,4},{4,0},{8,12},{12,8},{16,20},{20,16},{24,28},{28,24},{32,36},... | collective-permute-start | bytes 393224 | tf_op jit(solution)/shard_map/ppermute | solution.py:15
  20.2 0.8 fusion.102
  22.6 2.2 collective-permute-start.1
  24.8 0.9 reshape.730
  25.7 0.9 reshape_reshape.9
  26.9 0.9 reshape.732
  28.5 0.8 fusion.103
  29.4 0.8 convert_element_type.244
  31.4 0.9 copy.285
  32.4 0.8 rev.13
  33.2 1.0 copy.283
  35.3 1.1 convert_reduce_fusion.1
  36.9 0.9 convert_reduce_fusion.3
  39.2 1.0 fusion.1
  43.9 1.0 copy.311
  47.0 1.0 copy.317
  48.4 1.7 broadcast_select_fusion.9
  51.0 1.9 collective-permute-start.3
  52.9 1.0 maximum_convert_fusion
  54.6 3.6 %collective-permute-start.2 = (bf16[128,512]{1,0:T(8,128)(2,1)S(1)}, bf16[128,512]{1,0:T(8,128)(2,1)}, u32[]{:S(2)}, u32[]{:S(2)}) collective-permute-start(bf16[128,512]{1,0:T(8,128)(2,1)S(1)} %fusion.54), channel_id=1, source_target_pairs={{0,8},{4,12},{8,0},{12,4},{16,24},{20,28},{24,16},{28,20},{32,40},... | collective-permute-start | bytes 393224 | tf_op jit(solution)/shard_map/ppermute | solution.py:15
  59.1 1.9 collective-permute-start.5
  61.3 1.0 copy.323
  62.3 1.1 fusion.115
  64.0 0.9 broadcast_select_fusion.7
  67.5 4.0 %collective-permute-start.4 = (bf16[128,512]{1,0:T(8,128)(2,1)S(1)}, bf16[128,512]{1,0:T(8,128)(2,1)}, u32[]{:S(2)}, u32[]{:S(2)}) collective-permute-start(bf16[128,512]{1,0:T(8,128)(2,1)S(1)} %fusion.55), channel_id=1, source_target_pairs={{0,16},{4,20},{8,24},{12,28},{16,0},{20,4},{24,8},{28,12},{32,48},... | collective-permute-start | bytes 393224 | tf_op jit(solution)/shard_map/ppermute | solution.py:15
  71.5 1.3 fusion.99
  72.8 0.9 broadcast_select_fusion.1
  75.1 5.7 %collective-permute-start.7 = (bf16[128,512]{1,0:T(8,128)(2,1)}, bf16[128,512]{1,0:T(8,128)(2,1)}, u32[]{:S(2)}, u32[]{:S(2)}) collective-permute-start(bf16[128,512]{1,0:T(8,128)(2,1)} %bitcast.335), channel_id=1, source_target_pairs={{0,32},{4,36},{8,40},{12,44},{16,48},{20,52},{24,56},{28,60},{32,0... | collective-permute-start | bytes 393224 | tf_op jit(solution)/shard_map/ppermute | solution.py:15
  80.8 1.0 copy.341
  81.8 1.0 copy.335
  82.9 1.0 fusion.114
  85.6 0.9 broadcast_select_fusion.3
  87.5 3.5 %collective-permute-start.6 = (bf16[128,512]{1,0:T(8,128)(2,1)S(1)}, bf16[128,512]{1,0:T(8,128)(2,1)S(1)}, u32[]{:S(2)}, u32[]{:S(2)}) collective-permute-start(bf16[128,512]{1,0:T(8,128)(2,1)S(1)} %fusion.56), channel_id=1, source_target_pairs={{0,32},{4,36},{8,40},{12,44},{16,48},{20,52},{24,56},{28,60},{32,0... | collective-permute-start | bytes 393224 | tf_op jit(solution)/shard_map/ppermute | solution.py:15
  91.4 3.5 %collective-permute-done.7 = bf16[128,512]{1,0:T(8,128)(2,1)} collective-permute-done((bf16[128,512]{1,0:T(8,128)(2,1)}, bf16[128,512]{1,0:T(8,128)(2,1)}, u32[]{:S(2)}, u32[]{:S(2)}) %collective-permute-start.7) | collective-permute-done | bytes 131104 | tf_op jit(solution)/shard_map/ppermute | solution.py:15
  94.9 1.0 copy.351
  95.9 11.2 %collective-permute-done.6 = bf16[128,512]{1,0:T(8,128)(2,1)S(1)} collective-permute-done((bf16[128,512]{1,0:T(8,128)(2,1)S(1)}, bf16[128,512]{1,0:T(8,128)(2,1)S(1)}, u32[]{:S(2)}, u32[]{:S(2)}) %collective-permute-start.6) | collective-permute-done | bytes 131104 | tf_op jit(solution)/shard_map/ppermute | solution.py:15
  110.3 0.8 copy.354
  111.2 1.6 copy.297
  112.8 1.6 copy.314
  114.3 1.6 copy.326
  115.9 0.9 copy.338
  116.7 0.9 copy.350
  117.6 53.3 %all-gather.2.cloned.1.call-done = bf16[512,2048]{0,1:T(8,128)(2,1)} async-done(((bf16[512,16]{0,1:T(8,128)(2,1)}), bf16[512,2048]{0,1:T(8,128)(2,1)}) %all-gather.2.cloned.1.call-update) | async-done | bytes 2097168 | tf_op jit(solution)/shard_map/all_gather | solution.py:151
  171.1 1.6 mul.426
  179.8 3.5 %convolution_convert_fusion = bf16[512,2048]{1,0:T(8,128)(2,1)} fusion(bf16[512,2048]{0,1:T(8,128)(2,1)S(1)} %copy-done.2, f32[64,8,4,128]{3,2,1,0:T(4,128)S(1)} %bitcast.346, f32[64,8,4,128]{3,2,1,0:T(4,128)S(1)} %bitcast.341, f32[64,8,4,128]{3,2,1,0:T(4,128)S(1)} %bitcast.351, f32[64,8,4,128]{3,2,1,0:T(4,128)S(1)} %bitcast.336, ...), kind=kOutput, calls=%fused_computation | convolution fusion | flops 1079246848 | bytes 21102592 | tf_op jit(solution)/shard_map/dot_general | solution.py:149
  183.4 33.3 %reduce-scatter.2.cloned.1.call-done = bf16[512,512]{1,0:T(8,128)(2,1)} async-done(((bf16[512,2048]{1,0:T(8,128)(2,1)}), bf16[512,512]{1,0:T(8,128)(2,1)}) %reduce-scatter.2.cloned.1.call-update) | async-done | bytes 524304 | tf_op jit(solution)/shard_map/reduce_scatter | solution.py:155
  (199 shorter events, 35.1 us)
Async XLA Ops:
  6.5 164.4 %all-gather.2.cloned.1.call-start = ((), (), s32[]{:S(2)}) async-start(), calls=%async_computation.1 | async-start | bytes 2113536 | tf_op jit(solution)/shard_map/all_gather | solution.py:151
  7.3 209.4 %reduce-scatter.2.cloned.1.call-start = ((), (), s32[]{:S(2)}) async-start(), calls=%async_computation.2 | async-start | bytes 2621440 | tf_op jit(solution)/shard_map/reduce_scatter | solution.py:155
  9.8 9.7 %copy-start.1 = (bf16[512,512]{1,0:T(8,128)(2,1)S(1)}, bf16[512,512]{1,0:T(8,128)(2,1)}, u32[]{:S(2)}) copy-start(bf16[512,512]{1,0:T(8,128)(2,1)} %param.6) | copy-start | bytes 1572868
  10.7 33.1 %collective-permute-start = (bf16[128,512]{1,0:T(8,128)(2,1)S(1)}, bf16[128,512]{1,0:T(8,128)(2,1)}, u32[]{:S(2)}, u32[]{:S(2)}) collective-permute-start(bf16[128,512]{1,0:T(8,128)(2,1)S(1)} %fusion.53), channel_id=1, source_target_pairs={{0,4},{4,0},{8,12},{12,8},{16,20},{20,16},{24,28},{28,24},{32,36},... | collective-permute-start | bytes 393224 | tf_op jit(solution)/shard_map/ppermute | solution.py:15
  21.0 3.8 %copy-start = (bf16[512,512]{1,0:T(8,128)(2,1)S(1)}, bf16[512,512]{1,0:T(8,128)(2,1)}, u32[]{:S(2)}) copy-start(bf16[512,512]{1,0:T(8,128)(2,1)} %param.5) | copy-start | bytes 1572868
  22.6 4.4 %copy-start.3 = (bf16[512,512]{1,0:T(8,128)(2,1)S(1)}, bf16[512,512]{1,0:T(8,128)(2,1)}, u32[]{:S(2)}) copy-start(bf16[512,512]{1,0:T(8,128)(2,1)} %param.4) | copy-start | bytes 1572868
  22.6 24.5 %collective-permute-start.1 = (bf16[128,512]{1,0:T(8,128)(2,1)}, bf16[128,512]{1,0:T(8,128)(2,1)}, u32[]{:S(2)}, u32[]{:S(2)}) collective-permute-start(bf16[128,512]{1,0:T(8,128)(2,1)} %fusion.50), channel_id=1, source_target_pairs={{0,4},{4,0},{8,12},{12,8},{16,20},{20,16},{24,28},{28,24},{32,36},... | collective-permute-start | bytes 393224 | tf_op jit(solution)/shard_map/ppermute | solution.py:15
  29.3 2.1 copy-start.5
  29.3 3.0 %copy-start.4 = (bf16[2,2,128,4,128]{4,3,2,1,0:T(4,128)(2,1)S(1)}, bf16[2,2,128,4,128]{4,3,2,1,0:T(4,128)(2,1)}, u32[]{:S(2)}) copy-start(bf16[2,2,128,4,128]{4,3,2,1,0:T(4,128)(2,1)} %reshape_reshape.9) | copy-start | bytes 1572868
  34.6 3.1 %copy-start.11 = (bf16[1,2,128,4,128]{4,3,2,1,0:T(4,128)(2,1)S(1)}, bf16[1,2,128,4,128]{4,3,2,1,0:T(4,128)(2,1)}, u32[]{:S(2)}) copy-start(bf16[1,2,128,4,128]{4,3,2,1,0:T(4,128)(2,1)} %convert_element_type.246) | copy-start | bytes 786436
  34.6 3.2 %copy-start.12 = (bf16[2,128,4,128]{3,2,1,0:T(4,128)(2,1)S(1)}, bf16[2,128,4,128]{3,2,1,0:T(4,128)(2,1)}, u32[]{:S(2)}) copy-start(bf16[2,128,4,128]{3,2,1,0:T(4,128)(2,1)} %convert_element_type.244) | copy-start | bytes 786436
  36.8 1.8 copy-start.13
  36.8 1.8 copy-start.14
  36.8 1.8 copy-start.15
  38.7 1.5 copy-start.6
  51.0 7.3 %collective-permute-start.3 = (bf16[128,512]{1,0:T(8,128)(2,1)S(1)}, bf16[128,512]{1,0:T(8,128)(2,1)S(1)}, u32[]{:S(2)}, u32[]{:S(2)}) collective-permute-start(bf16[128,512]{1,0:T(8,128)(2,1)S(1)} %fusion.51), channel_id=1, source_target_pairs={{0,8},{4,12},{8,0},{12,4},{16,24},{20,28},{24,16},{28,20},{32,40},... | collective-permute-start | bytes 393224 | tf_op jit(solution)/shard_map/ppermute | solution.py:15
  54.6 6.6 %collective-permute-start.2 = (bf16[128,512]{1,0:T(8,128)(2,1)S(1)}, bf16[128,512]{1,0:T(8,128)(2,1)}, u32[]{:S(2)}, u32[]{:S(2)}) collective-permute-start(bf16[128,512]{1,0:T(8,128)(2,1)S(1)} %fusion.54), channel_id=1, source_target_pairs={{0,8},{4,12},{8,0},{12,4},{16,24},{20,28},{24,16},{28,20},{32,40},... | collective-permute-start | bytes 393224 | tf_op jit(solution)/shard_map/ppermute | solution.py:15
  59.1 13.7 %collective-permute-start.5 = (bf16[128,512]{1,0:T(8,128)(2,1)S(1)}, bf16[128,512]{1,0:T(8,128)(2,1)}, u32[]{:S(2)}, u32[]{:S(2)}) collective-permute-start(bf16[128,512]{1,0:T(8,128)(2,1)S(1)} %fusion.52), channel_id=1, source_target_pairs={{0,16},{4,20},{8,24},{12,28},{16,0},{20,4},{24,8},{28,12},{32,48},... | collective-permute-start | bytes 393224 | tf_op jit(solution)/shard_map/ppermute | solution.py:15
  67.5 14.4 %collective-permute-start.4 = (bf16[128,512]{1,0:T(8,128)(2,1)S(1)}, bf16[128,512]{1,0:T(8,128)(2,1)}, u32[]{:S(2)}, u32[]{:S(2)}) collective-permute-start(bf16[128,512]{1,0:T(8,128)(2,1)S(1)} %fusion.55), channel_id=1, source_target_pairs={{0,16},{4,20},{8,24},{12,28},{16,0},{20,4},{24,8},{28,12},{32,48},... | collective-permute-start | bytes 393224 | tf_op jit(solution)/shard_map/ppermute | solution.py:15
  75.1 19.7 %collective-permute-start.7 = (bf16[128,512]{1,0:T(8,128)(2,1)}, bf16[128,512]{1,0:T(8,128)(2,1)}, u32[]{:S(2)}, u32[]{:S(2)}) collective-permute-start(bf16[128,512]{1,0:T(8,128)(2,1)} %bitcast.335), channel_id=1, source_target_pairs={{0,32},{4,36},{8,40},{12,44},{16,48},{20,52},{24,56},{28,60},{32,0... | collective-permute-start | bytes 393224 | tf_op jit(solution)/shard_map/ppermute | solution.py:15
  83.9 2.6 %copy-start.22 = (f32[4,32]{1,0:T(4,128)}, f32[4,32]{1,0:T(4,128)S(1)}, u32[]{:S(2)}) copy-start(f32[4,32]{1,0:T(4,128)S(1)} %get-tuple-element.60) | copy-start | bytes 1540
  86.5 20.7 %copy-start.20 = (bf16[16,512]{1,0:T(8,128)(2,1)S(1)}, bf16[16,512]{1,0:T(8,128)(2,1)}, u32[]{:S(2)}) copy-start(bf16[16,512]{1,0:T(8,128)(2,1)} %convert_reduce_fusion.4) | copy-start | bytes 49156
  86.6 4.4 %copy-start.23 = (f32[4,32]{1,0:T(4,128)S(1)}, f32[4,32]{1,0:T(4,128)}, u32[]{:S(2)}) copy-start(f32[4,32]{1,0:T(4,128)} %copy-done.22) | copy-start | bytes 1540
  86.6 22.2 %copy-start.18 = (f32[512,4]{0,1:T(4,128)S(1)}, f32[512,4]{0,1:T(4,128)}, u32[]{:S(2)}) copy-start(f32[512,4]{0,1:T(4,128)} %reshape.749) | copy-start | bytes 24580
  86.6 22.2 %copy-start.19 = (f32[512,4]{0,1:T(4,128)S(1)}, f32[512,4]{0,1:T(4,128)}, u32[]{:S(2)}) copy-start(f32[512,4]{0,1:T(4,128)} %reshape.755) | copy-start | bytes 24580
  86.6 22.2 %copy-start.21 = (f32[4,4,128]{2,1,0:T(4,128)S(1)}, f32[4,4,128]{2,1,0:T(4,128)}, u32[]{:S(2)}) copy-start(f32[4,4,128]{2,1,0:T(4,128)} %fusion.1) | copy-start | bytes 24580
  86.6 22.2 %copy-start.24 = (f32[512,4]{0,1:T(4,128)S(1)}, f32[512,4]{0,1:T(4,128)}, u32[]{:S(2)}) copy-start(f32[512,4]{0,1:T(4,128)} %copy.356) | copy-start | bytes 24580
  86.6 22.2 %copy-start.25 = (f32[512,4]{0,1:T(4,128)S(1)}, f32[512,4]{0,1:T(4,128)}, u32[]{:S(2)}) copy-start(f32[512,4]{0,1:T(4,128)} %reshape.775) | copy-start | bytes 24580
  87.0 21.9 %copy-start.26 = (f32[512,4]{0,1:T(4,128)S(1)}, f32[512,4]{0,1:T(4,128)}, u32[]{:S(2)}) copy-start(f32[512,4]{0,1:T(4,128)} %reshape.777) | copy-start | bytes 24580
  87.0 21.9 %copy-start.27 = (f32[512,4]{0,1:T(4,128)S(1)}, f32[512,4]{0,1:T(4,128)}, u32[]{:S(2)}) copy-start(f32[512,4]{0,1:T(4,128)} %reshape.761) | copy-start | bytes 24580
  87.0 21.9 %copy-start.30 = (f32[512,4]{0,1:T(4,128)S(1)}, f32[512,4]{0,1:T(4,128)}, u32[]{:S(2)}) copy-start(f32[512,4]{0,1:T(4,128)} %get-tuple-element.18) | copy-start | bytes 24580
  87.0 21.9 %copy-start.31 = (f32[512,4]{0,1:T(4,128)S(1)}, f32[512,4]{0,1:T(4,128)}, u32[]{:S(2)}) copy-start(f32[512,4]{0,1:T(4,128)} %get-tuple-element.19) | copy-start | bytes 24580
  87.5 19.6 %collective-permute-start.6 = (bf16[128,512]{1,0:T(8,128)(2,1)S(1)}, bf16[128,512]{1,0:T(8,128)(2,1)S(1)}, u32[]{:S(2)}, u32[]{:S(2)}) collective-permute-start(bf16[128,512]{1,0:T(8,128)(2,1)S(1)} %fusion.56), channel_id=1, source_target_pairs={{0,32},{4,36},{8,40},{12,44},{16,48},{20,52},{24,56},{28,60},{32,0... | collective-permute-start | bytes 393224 | tf_op jit(solution)/shard_map/ppermute | solution.py:15
  109.6 6.3 %copy-start.29 = (f32[512,4]{0,1:T(4,128)S(1)}, f32[512,4]{0,1:T(4,128)}, u32[]{:S(2)}) copy-start(f32[512,4]{0,1:T(4,128)} %get-tuple-element.14) | copy-start | bytes 24580
  109.6 7.2 %copy-start.28 = (f32[512,4]{0,1:T(4,128)S(1)}, f32[512,4]{0,1:T(4,128)}, u32[]{:S(2)}) copy-start(f32[512,4]{0,1:T(4,128)} %get-tuple-element.15) | copy-start | bytes 24580
  170.9 1.8 copy-start.10
  170.9 2.4 %copy-start.9 = (f32[512,4]{1,0:T(8,128)S(1)}, f32[512,4]{1,0:T(8,128)}, u32[]{:S(2)}) copy-start(f32[512,4]{1,0:T(8,128)} %copy.326) | copy-start | bytes 24580
  171.1 2.8 %copy-start.8 = (f32[512,4]{1,0:T(8,128)S(1)}, f32[512,4]{1,0:T(8,128)}, u32[]{:S(2)}) copy-start(f32[512,4]{1,0:T(8,128)} %copy.314) | copy-start | bytes 24580
  172.7 1.8 copy-start.7
  177.6 1.4 copy-start.16
  178.2 0.9 copy-start.17
  178.2 1.6 copy-start.2
Sparse Core Ops, SparseCore 0:
  10.5 160.4 all-gather.1
  183.5 33.1 reduce-scatter.1
where the time goes:
time: 224 us; the launch traced here: 223 us
  waiting for transfers between devices  102 us (46%)
  local copies, waits for them, and re-layouts  52.1 us (23%)
  starting transfers between devices  31.7 us (14%)
  between operations  14.6 us (7%)
  other arithmetic  14.2 us (6%)
  matrix products  8.56 us (4%)
    all_gather x1, waiting for transfers between devices, body(): lax.all_gather(out_weight, 'seq', axis=1, tiled=True)  53.3 us
    reduce_scatter x1, waiting for transfers between devices, body(): lax.psum_scatter(rounded_terms.astype(jnp.bfloat16), 'head', scatter_dime...  33.3 us
    ppermute x8, starting transfers between devices, partner(): return lax.ppermute(value, axis, pairs)  31.6 us
    ppermute x8, waiting for transfers between devices, partner(): return lax.ppermute(value, axis, pairs)  15 us
    exp x5, local copies, waits for them, and re-layouts, merge_level(): keep_old = jnp.exp(running_max - newest)  6.4 us
    ppermute x8, local copies, waits for them, and re-layouts, partner(): return lax.ppermute(value, axis, pairs)  6.36 us
  transfers between devices with their start and end apart: 10, of which 5 were waited for; matrix products, arithmetic and copies ran while one was open for 28% of the time, Pallas kernels for 0%

commit v1 on v0

--- a/solution.py
+++ b/solution.py
@@ -7,6 +7,11 @@
 HEAD_DIM = 128
 BLOCK = 128
 LEVELS = 5
+
+
+def _group_members_all(block_here, net_axis, ndim_at):
+    v_next = jnp.concatenate(jax.lax.all_gather(block_here, net_axis), ndim_at)
+    return v_next
 
 
 def partner(value, axis, stride):
@@ -148,7 +153,7 @@
     )
     partial_terms = jnp.dot(
         attended,
-        lax.all_gather(out_weight, "seq", axis=1, tiled=True),
+        _group_members_all(out_weight, "seq", ndim_at=1),
         preferred_element_type=jnp.float32,
     )
     rounded_terms = partial_terms.astype(jnp.bfloat16).astype(jnp.float32)

time: 224 us -> 220 us (0.982)
  local copies, waits for them, and re-layouts: 52.1 us -> 32.7 us
  waiting for transfers between devices: 102 us -> 119 us
    all_gather x1, waiting for transfers between devices: 53.3 us -> 66.1 us  [_group_members_all(): v_next = jnp.concatenate(jax.lax.all_gather(block_here, net_axis), ndim_at)]
    exp x10 -> x0, local copies, waits for them, and re-layouts: 7.84 us -> none  [the longest x5 6.4 us: merge_level(): keep_old = jnp.exp(running_max - newest)]
    mul x10 -> x0, local copies, waits for them, and re-layouts: 7.01 us -> none  [the longest x5 3.99 us: merge_level(): running_out * keep_old[..., None] + weighted_value_sum * keep_new[..., None]]
    ppermute x8, waiting for transfers between devices: 15 us -> 19.7 us  [partner(): return lax.ppermute(value, axis, pairs)]
    convert_element_type x0 -> x1, other arithmetic: none -> 3.77 us  [body(): (running[2] / running[1][..., None]).reshape(row_count, col_count)]
    ppermute x8, local copies, waits for them, and re-layouts: 6.36 us -> 3.65 us  [partner(): return lax.ppermute(value, axis, pairs)]
  transfers between devices with their start and end apart: 10 -> 10, of which waited for: 5 -> 5; matrix products, arithmetic and copies ran while one was open for 28% -> 20% of each run, Pallas kernels for 0% -> 0%
where the time goes in v1:
time: 220 us; the launch traced here: 219 us
  waiting for transfers between devices  119 us (54%)
  local copies, waits for them, and re-layouts  32.7 us (15%)
  starting transfers between devices  31.5 us (14%)
  between operations  14.4 us (7%)
  other arithmetic  12.9 us (6%)
  matrix products  9.13 us (4%)
    all_gather x1, waiting for transfers between devices, _group_members_all(): v_next = jnp.concatenate(jax.lax.all_gather(block_here, net_axis), ndim_at)  66.1 us
    reduce_scatter x1, waiting for transfers between devices, body(): lax.psum_scatter(rounded_terms.astype(jnp.bfloat16), 'head', scatter_dime...  32.8 us
    ppermute x8, starting transfers between devices, partner(): return lax.ppermute(value, axis, pairs)  31.3 us
    ppermute x8, waiting for transfers between devices, partner(): return lax.ppermute(value, axis, pairs)  19.7 us
    dot_general x6, matrix products, level_terms(): jnp.einsum('bqhd,bkhd->bhqk', blocked_query_rows, blocked_key_rows, prefe...  4.7 us
  transfers between devices with their start and end apart: 10, of which 5 were waited for; matrix products, arithmetic and copies ran while one was open for 20% of the time, Pallas kernels for 0%

profile of v1, /device:TPU:1, one launch (start us, length us, event | category | flops | bytes accessed | tf_op | source)
XLA Modules:
  0.0 219.4 jit_solution(11495291317112412173)
XLA Ops:
  6.5 1.7 reshape.872
  8.2 0.8 fusion.106
  10.0 8.7 %collective-permute-start = (bf16[128,512]{1,0:T(8,128)(2,1)S(1)}, bf16[128,512]{1,0:T(8,128)(2,1)}, u32[]{:S(2)}, u32[]{:S(2)}) collective-permute-start(bf16[128,512]{1,0:T(8,128)(2,1)S(1)} %fusion.57), channel_id=1, source_target_pairs={{0,4},{4,0},{8,12},{12,8},{16,20},{20,16},{24,28},{28,24},{32,36},... | collective-permute-start | bytes 393224 | tf_op jit(solution)/shard_map/ppermute | solution.py:20
  18.7 0.7 reshape.874
  19.4 0.8 fusion.108
  21.1 0.7 fusion.54
  21.8 1.9 collective-permute-start.1
  24.0 0.8 convert_element_type.255
  24.7 0.7 reshape.870
  25.4 0.8 fusion.107
  26.3 1.1 reshape.875
  27.6 0.9 reshape_reshape.9
  28.6 0.9 reshape.817
  29.5 0.8 convert_element_type.257
  31.2 1.1 convert_reduce_fusion.1
  32.8 1.4 convert_reduce_fusion.3
  34.1 0.8 reverse_bitcast_fusion.1
  35.1 0.8 rev.13
  35.9 0.9 copy.231
  37.9 1.8 bitcast_reduce_fusion
  39.7 1.0 fusion.1
  40.7 0.6 convolution_bitcast_fusion
  42.5 0.7 copy.288
  43.3 0.7 convert_reduce_fusion.4
  44.0 1.1 broadcast_select_fusion.9
  45.9 1.9 collective-permute-start.2
  48.7 3.4 %collective-permute-start.3 = (bf16[128,512]{1,0:T(8,128)(2,1)S(1)}, bf16[128,512]{1,0:T(8,128)(2,1)S(1)}, u32[]{:S(2)}, u32[]{:S(2)}) collective-permute-start(bf16[128,512]{1,0:T(8,128)(2,1)S(1)} %fusion.55), channel_id=1, source_target_pairs={{0,8},{4,12},{8,0},{12,4},{16,24},{20,28},{24,16},{28,20},{32,40},... | collective-permute-start | bytes 393224 | tf_op jit(solution)/shard_map/ppermute | solution.py:20
  52.1 1.0 copy.254
  53.5 0.8 reshape.834
  54.5 0.8 reshape.860
  55.2 1.0 copy.259
  57.5 2.1 collective-permute-start.5
  60.5 4.3 %collective-permute-start.4 = (bf16[128,512]{1,0:T(8,128)(2,1)S(1)}, bf16[128,512]{1,0:T(8,128)(2,1)S(1)}, u32[]{:S(2)}, u32[]{:S(2)}) collective-permute-start(bf16[128,512]{1,0:T(8,128)(2,1)S(1)} %fusion.59), channel_id=1, source_target_pairs={{0,16},{4,20},{8,24},{12,28},{16,0},{20,4},{24,8},{28,12},{32,48},... | collective-permute-start | bytes 393224 | tf_op jit(solution)/shard_map/ppermute | solution.py:20
  64.9 1.1 fusion.121
  66.3 0.7 reshape.862
  67.6 0.6 fusion.103
  68.2 2.8 %collective-permute-done.5 = bf16[128,512]{1,0:T(8,128)(2,1)S(1)} collective-permute-done((bf16[128,512]{1,0:T(8,128)(2,1)S(1)}, bf16[128,512]{1,0:T(8,128)(2,1)S(1)}, u32[]{:S(2)}, u32[]{:S(2)}) %collective-permute-start.5) | collective-permute-done | bytes 131104 | tf_op jit(solution)/shard_map/ppermute | solution.py:20
  71.7 1.9 collective-permute-start.7
  74.8 7.1 %collective-permute-start.6 = (bf16[128,512]{1,0:T(8,128)(2,1)S(1)}, bf16[128,512]{1,0:T(8,128)(2,1)S(1)}, u32[]{:S(2)}, u32[]{:S(2)}) collective-permute-start(bf16[128,512]{1,0:T(8,128)(2,1)S(1)} %fusion.60), channel_id=1, source_target_pairs={{0,32},{4,36},{8,40},{12,44},{16,48},{20,52},{24,56},{28,60},{32,0... | collective-permute-start | bytes 393224 | tf_op jit(solution)/shard_map/ppermute | solution.py:20
  82.0 1.0 fusion.120
  83.9 16.7 %collective-permute-done.6 = bf16[128,512]{1,0:T(8,128)(2,1)S(1)} collective-permute-done((bf16[128,512]{1,0:T(8,128)(2,1)S(1)}, bf16[128,512]{1,0:T(8,128)(2,1)S(1)}, u32[]{:S(2)}, u32[]{:S(2)}) %collective-permute-start.6) | collective-permute-done | bytes 131104 | tf_op jit(solution)/shard_map/ppermute | solution.py:20
  101.5 1.0 copy.285
  103.5 3.8 %fusion.13 = bf16[512,4,128]{2,0,1:T(8,128)(2,1)S(1)} fusion(f32[4,128,4,128]{3,1,0,2:T(8,128)S(1)} %copy.234, f32[512,4,128]{2,0,1:T(8,128)S(1)} %bitcast.280, f32[512,4,128]{2,0,1:T(8,128)S(1)} %bitcast.281, f32[512,4]{0,1:T(4,128)S(1)} %get-tuple-element.5, f32[512,4]{0,1:T(4,128)S(1)} %get-tuple-element.10, ...), kind=kLoop, calls=%fused_computation.27 | loop fusion | flops 4456448 | bytes 3989504 | tf_op jit(solution)/shard_map/convert_element_type | solution.py:152
  107.5 66.1 %all-gather.3.cloned.1.call-done = bf16[65536,16]{0,1:T(8,128)(2,1)} async-done(((bf16[512,16]{0,1:T(8,128)(2,1)}), bf16[65536,16]{0,1:T(8,128)(2,1)}) %all-gather.3.cloned.1.call-update) | async-done | bytes 2097168 | tf_op jit(solution)/shard_map/all_gather | solution.py:13
  173.6 2.3 %copy.330 = bf16[2,8,128,512]{3,2,1,0:T(8,128)(2,1)S(1)} copy(bf16[2,8,128,512]{3,1,2,0:T(8,128)(2,1)} %bitcast.283) | data formatting | bytes 4194304
  175.8 1.2 copy.290
  177.0 2.7 %convolution_convert_fusion = bf16[512,2048]{1,0:T(8,128)(2,1)} fusion(bf16[512,512]{0,1:T(8,128)(2,1)S(1)} %bitcast.292, bf16[512,2048]{0,1:T(8,128)(2,1)S(1)} %bitcast.284), kind=kOutput, calls=%fused_computation | convolution fusion | flops 1074790400 | bytes 4718592 | tf_op jit(solution)/shard_map/dot_general | solution.py:154
  179.7 32.8 %reduce-scatter.2.cloned.1.call-done = bf16[512,512]{1,0:T(8,128)(2,1)} async-done(((bf16[512,2048]{1,0:T(8,128)(2,1)}), bf16[512,512]{1,0:T(8,128)(2,1)}) %reduce-scatter.2.cloned.1.call-update) | async-done | bytes 524304 | tf_op jit(solution)/shard_map/reduce_scatter | solution.py:160
  (151 shorter events, 15.8 us)
Async XLA Ops:
  6.5 167.0 %all-gather.3.cloned.1.call-start = ((), (), s32[]{:S(2)}) async-start(), calls=%async_computation.2 | async-start | bytes 2113536 | tf_op jit(solution)/shard_map/all_gather | solution.py:13
  9.1 9.7 %copy-start.1 = (bf16[512,512]{1,0:T(8,128)(2,1)S(1)}, bf16[512,512]{1,0:T(8,128)(2,1)}, u32[]{:S(2)}) copy-start(bf16[512,512]{1,0:T(8,128)(2,1)} %param.6) | copy-start | bytes 1572868
  10.0 34.1 %collective-permute-start = (bf16[128,512]{1,0:T(8,128)(2,1)S(1)}, bf16[128,512]{1,0:T(8,128)(2,1)}, u32[]{:S(2)}, u32[]{:S(2)}) collective-permute-start(bf16[128,512]{1,0:T(8,128)(2,1)S(1)} %fusion.57), channel_id=1, source_target_pairs={{0,4},{4,0},{8,12},{12,8},{16,20},{20,16},{24,28},{28,24},{32,36},... | collective-permute-start | bytes 393224 | tf_op jit(solution)/shard_map/ppermute | solution.py:20
  20.2 4.5 %copy-start.2 = (bf16[512,512]{1,0:T(8,128)(2,1)S(1)}, bf16[512,512]{1,0:T(8,128)(2,1)}, u32[]{:S(2)}) copy-start(bf16[512,512]{1,0:T(8,128)(2,1)} %param.4) | copy-start | bytes 1572868
  21.8 22.2 %collective-permute-start.1 = (bf16[128,512]{1,0:T(8,128)(2,1)}, bf16[128,512]{1,0:T(8,128)(2,1)}, u32[]{:S(2)}, u32[]{:S(2)}) collective-permute-start(bf16[128,512]{1,0:T(8,128)(2,1)} %fusion.54), channel_id=1, source_target_pairs={{0,4},{4,0},{8,12},{12,8},{16,20},{20,16},{24,28},{28,24},{32,36},... | collective-permute-start | bytes 393224 | tf_op jit(solution)/shard_map/ppermute | solution.py:20
  23.7 188.8 %reduce-scatter.2.cloned.1.call-start = ((), (), s32[]{:S(2)}) async-start(), calls=%async_computation.1 | async-start | bytes 2621440 | tf_op jit(solution)/shard_map/reduce_scatter | solution.py:160
  25.4 2.2 copy-start
  28.6 2.0 copy-start.4
  30.6 3.6 %copy-start.5 = (bf16[1,2,128,4,128]{4,3,2,1,0:T(4,128)(2,1)S(1)}, bf16[1,2,128,4,128]{4,3,2,1,0:T(4,128)(2,1)}, u32[]{:S(2)}) copy-start(bf16[1,2,128,4,128]{4,3,2,1,0:T(4,128)(2,1)} %convert_element_type.255) | copy-start | bytes 786436
  30.6 4.3 %copy-start.3 = (bf16[2,2,128,4,128]{4,3,2,1,0:T(4,128)(2,1)S(1)}, bf16[2,2,128,4,128]{4,3,2,1,0:T(4,128)(2,1)}, u32[]{:S(2)}) copy-start(bf16[2,2,128,4,128]{4,3,2,1,0:T(4,128)(2,1)} %reshape_reshape.9) | copy-start | bytes 1572868
  35.0 1.8 copy-start.7
  35.0 2.2 copy-start.6
  40.7 0.8 copy-start.8
  45.9 13.7 %collective-permute-start.2 = (bf16[128,512]{1,0:T(8,128)(2,1)S(1)}, bf16[128,512]{1,0:T(8,128)(2,1)S(1)}, u32[]{:S(2)}, u32[]{:S(2)}) collective-permute-start(bf16[128,512]{1,0:T(8,128)(2,1)S(1)} %fusion.58), channel_id=1, source_target_pairs={{0,8},{4,12},{8,0},{12,4},{16,24},{20,28},{24,16},{28,20},{32,40},... | collective-permute-start | bytes 393224 | tf_op jit(solution)/shard_map/ppermute | solution.py:20
  48.7 7.9 %collective-permute-start.3 = (bf16[128,512]{1,0:T(8,128)(2,1)S(1)}, bf16[128,512]{1,0:T(8,128)(2,1)S(1)}, u32[]{:S(2)}, u32[]{:S(2)}) collective-permute-start(bf16[128,512]{1,0:T(8,128)(2,1)S(1)} %fusion.55), channel_id=1, source_target_pairs={{0,8},{4,12},{8,0},{12,4},{16,24},{20,28},{24,16},{28,20},{32,40},... | collective-permute-start | bytes 393224 | tf_op jit(solution)/shard_map/ppermute | solution.py:20
  57.5 13.5 %collective-permute-start.5 = (bf16[128,512]{1,0:T(8,128)(2,1)S(1)}, bf16[128,512]{1,0:T(8,128)(2,1)S(1)}, u32[]{:S(2)}, u32[]{:S(2)}) collective-permute-start(bf16[128,512]{1,0:T(8,128)(2,1)S(1)} %fusion.56), channel_id=1, source_target_pairs={{0,16},{4,20},{8,24},{12,28},{16,0},{20,4},{24,8},{28,12},{32,48},... | collective-permute-start | bytes 393224 | tf_op jit(solution)/shard_map/ppermute | solution.py:20
  60.0 7.6 %copy-start.9 = (f32[512,4]{0,1:T(4,128)S(1)}, f32[512,4]{0,1:T(4,128)}, u32[]{:S(2)}) copy-start(f32[512,4]{0,1:T(4,128)} %reshape.834) | copy-start | bytes 24580
  60.5 13.4 %collective-permute-start.4 = (bf16[128,512]{1,0:T(8,128)(2,1)S(1)}, bf16[128,512]{1,0:T(8,128)(2,1)S(1)}, u32[]{:S(2)}, u32[]{:S(2)}) collective-permute-start(bf16[128,512]{1,0:T(8,128)(2,1)S(1)} %fusion.59), channel_id=1, source_target_pairs={{0,16},{4,20},{8,24},{12,28},{16,0},{20,4},{24,8},{28,12},{32,48},... | collective-permute-start | bytes 393224 | tf_op jit(solution)/shard_map/ppermute | solution.py:20
  67.2 4.2 %copy-start.11 = (f32[512,4]{0,1:T(4,128)}, f32[512,4]{0,1:T(4,128)S(1)}, u32[]{:S(2)}) copy-start(f32[512,4]{0,1:T(4,128)S(1)} %reshape.840) | copy-start | bytes 24580
  71.7 29.8 %collective-permute-start.7 = (bf16[128,512]{1,0:T(8,128)(2,1)S(1)}, bf16[128,512]{1,0:T(8,128)(2,1)}, u32[]{:S(2)}, u32[]{:S(2)}) collective-permute-start(bf16[128,512]{1,0:T(8,128)(2,1)S(1)} %bitcast.299), channel_id=1, source_target_pairs={{0,32},{4,36},{8,40},{12,44},{16,48},{20,52},{24,56},{28,60},{32,0... | collective-permute-start | bytes 393224 | tf_op jit(solution)/shard_map/ppermute | solution.py:20
  74.0 26.8 %copy-start.13 = (bf16[16,512]{1,0:T(8,128)(2,1)S(1)}, bf16[16,512]{1,0:T(8,128)(2,1)}, u32[]{:S(2)}) copy-start(bf16[16,512]{1,0:T(8,128)(2,1)} %convert_reduce_fusion.4) | copy-start | bytes 49156
  74.3 28.5 %copy-start.10 = (f32[512,4]{0,1:T(4,128)S(1)}, f32[512,4]{0,1:T(4,128)}, u32[]{:S(2)}) copy-start(f32[512,4]{0,1:T(4,128)} %reshape.834) | copy-start | bytes 24580
  74.3 28.5 %copy-start.12 = (f32[512,4]{0,1:T(4,128)S(1)}, f32[512,4]{0,1:T(4,128)}, u32[]{:S(2)}) copy-start(f32[512,4]{0,1:T(4,128)} %copy-done.11) | copy-start | bytes 24580
  74.3 28.5 %copy-start.14 = (f32[4,4,128]{2,1,0:T(4,128)S(1)}, f32[4,4,128]{2,1,0:T(4,128)}, u32[]{:S(2)}) copy-start(f32[4,4,128]{2,1,0:T(4,128)} %fusion.1) | copy-start | bytes 24580
  74.3 28.5 %copy-start.15 = (f32[512,4]{0,1:T(4,128)S(1)}, f32[512,4]{0,1:T(4,128)}, u32[]{:S(2)}) copy-start(f32[512,4]{0,1:T(4,128)} %copy.288) | copy-start | bytes 24580
  74.3 28.5 %copy-start.16 = (f32[512,4]{0,1:T(4,128)S(1)}, f32[512,4]{0,1:T(4,128)}, u32[]{:S(2)}) copy-start(f32[512,4]{0,1:T(4,128)} %reshape.860) | copy-start | bytes 24580
  74.4 28.5 %copy-start.17 = (f32[512,4]{0,1:T(4,128)S(1)}, f32[512,4]{0,1:T(4,128)}, u32[]{:S(2)}) copy-start(f32[512,4]{0,1:T(4,128)} %reshape.862) | copy-start | bytes 24580
  74.4 28.5 %copy-start.18 = (f32[512,4]{0,1:T(4,128)S(1)}, f32[512,4]{0,1:T(4,128)}, u32[]{:S(2)}) copy-start(f32[512,4]{0,1:T(4,128)} %get-tuple-element.18) | copy-start | bytes 24580
  74.4 28.5 %copy-start.19 = (f32[512,4]{0,1:T(4,128)S(1)}, f32[512,4]{0,1:T(4,128)}, u32[]{:S(2)}) copy-start(f32[512,4]{0,1:T(4,128)} %get-tuple-element.19) | copy-start | bytes 24580
  74.8 25.8 %collective-permute-start.6 = (bf16[128,512]{1,0:T(8,128)(2,1)S(1)}, bf16[128,512]{1,0:T(8,128)(2,1)S(1)}, u32[]{:S(2)}, u32[]{:S(2)}) collective-permute-start(bf16[128,512]{1,0:T(8,128)(2,1)S(1)} %fusion.60), channel_id=1, source_target_pairs={{0,32},{4,36},{8,40},{12,44},{16,48},{20,52},{24,56},{28,60},{32,0... | collective-permute-start | bytes 393224 | tf_op jit(solution)/shard_map/ppermute | solution.py:20
Sparse Core Ops, SparseCore 0:
  23.9 149.6 all-gather.2
  179.8 32.6 reduce-scatter.1
